TPU v7x, 256 devices: a whole 4x4x8 slice. The times are simulated.
256 devices in a mesh: row: 8 (over y, core), col: 8 (over x, z_hi), rep: 4 (over z_lo).
Axes of the slice: x: 4, y: 4, z: 8 (z_hi: 2, z_lo: 4; z = z_hi * 4 + z_lo), core: 2. Of those that a mesh axis runs over, the one named last changes fastest.
Arguments:
- features: float32 [256, 32768], P('rep', ('col', 'row')), may hold values from -6 to 6
- weight: float32 [256, 256], replicated, may hold values from -0.375 to 0.375
- cotangent: float32 [256, 32768], P('rep', ('row', 'col')), may hold values from -6 to 6
- tile_values: float32 [10240, 128, 128], P(('row', 'col')), may hold values from -0.078125 to 0.078125
- tile_row: int32 [10240], P(('row', 'col')), may hold values from 0 to 31
- tile_col: int32 [10240], P(('row', 'col')), may hold values from 0 to 31
- tile_kind: int32 [10240], P(('row', 'col')), may hold values from 0 to 159
- tile_count: int32 [64], P(('row', 'col')), may hold values from 40 to 160, as said below
Outputs:
- output: float32 [256, 32768], P('rep', ('row', 'col'))
- input_grad: float32 [256, 32768], P('rep', ('col', 'row'))
- weight_grad: float32 [256, 256], P('rep')
Inputs may be any that keep to these rules, and one draw needn't show every extreme that they name: `tile_count`: a block's slots at or after its count are not part of the adjacency; some block uses all 160 slots. `tile_row`: slots may repeat a tile position; their tiles add. `tile_kind`: an index into the 160 stored tiles of the same block.
All inputs are finite; a program needn't handle non-finite values.
Results may differ from a plain program's by a relative error of at most 0.0001.
Values sent between devices are 32-bit elements; how exact they have to be, the bound alone decides.
No kernel may reach another device: no remote copies, remote signals or barrier semaphores. Data moves between devices by JAX's collectives and lax.ppermute only.
A program may use at most 128 MiB of HBM per device.

v0:
```python
import jax
import jax.numpy as jnp
from jax import lax
from jax.sharding import PartitionSpec as P


def tile_terms(source, values, from_tile, to_tile, tile_kinds, live_weight, dest_tiles, transposed):
    feat_width = source.shape[0]
    tile_edge = values.shape[1]
    tiled = source.reshape(feat_width, source.shape[1] // tile_edge, tile_edge)
    picked = jnp.take(tiled, from_tile, axis=1)
    chosen = jnp.take(values, tile_kinds, axis=0)
    if transposed:
        products = jnp.einsum("fga,gab->fgb", picked, chosen, precision=lax.Precision.HIGHEST)
    else:
        products = jnp.einsum("fgb,gab->fga", picked, chosen, precision=lax.Precision.HIGHEST)
    onehot = (to_tile[:, None] == jnp.arange(dest_tiles, dtype=jnp.int32)[None, :]).astype(
        jnp.float32
    )
    onehot = onehot * live_weight[:, None]
    spread = jnp.einsum("fgt,gd->fdt", products, onehot, precision=lax.Precision.HIGHEST)
    return spread.reshape(feat_width, dest_tiles * tile_edge)


def aggregate(source, values, from_tile, to_tile, tile_kinds, live_count, dest_tiles, transposed):
    slot_total = tile_kinds.shape[0]
    live_weight = (jnp.arange(slot_total, dtype=jnp.int32) < live_count).astype(jnp.float32)
    return tile_terms(
        source, values, from_tile, to_tile, tile_kinds, live_weight, dest_tiles, transposed
    )


def local(features, weight, cotangent, tile_values, tile_row, tile_col, tile_kind, tile_count):
    n_rowdev = lax.axis_size("row")
    n_coldev = lax.axis_size("col")
    n_repdev = lax.axis_size("rep")
    quarter = weight.shape[0] // n_repdev
    rep_index = lax.axis_index("rep")
    own_rows = lax.dynamic_slice_in_dim(weight, rep_index * quarter, quarter, 0)
    own_cols = lax.dynamic_slice_in_dim(weight, rep_index * quarter, quarter, 1)
    stretch_len = features.shape[1]
    tile_edge = tile_values.shape[1]
    live_count = tile_count[0]
    row_tiles = n_coldev * stretch_len // tile_edge
    col_tiles = n_rowdev * stretch_len // tile_edge
    mixed = lax.psum_scatter(
        lax.dot_general(
            own_rows,
            features,
            (((0,), (0,)), ((), ())),
            precision=lax.Precision.HIGHEST,
            preferred_element_type=jnp.float32,
        ),
        "rep",
        scatter_dimension=0,
        tiled=True,
    )
    column_block = lax.all_gather(mixed, "row", axis=1, tiled=True)
    partial_value = aggregate(
        column_block, tile_values, tile_col, tile_row, tile_kind, live_count, row_tiles, False
    )
    summed = lax.psum_scatter(partial_value, "col", scatter_dimension=1, tiled=True)
    output, pullback = jax.vjp(lambda v: jax.nn.gelu(v, approximate=True), summed)
    (grad_pre,) = pullback(cotangent)
    row_block = lax.all_gather(grad_pre, "col", axis=1, tiled=True)
    partial_back = aggregate(
        row_block, tile_values, tile_row, tile_col, tile_kind, live_count, col_tiles, True
    )
    grad_mixed = lax.psum_scatter(partial_back, "row", scatter_dimension=1, tiled=True)
    input_grad = lax.psum_scatter(
        jnp.dot(
            own_cols,
            grad_mixed,
            preferred_element_type=jnp.float32,
            precision=lax.Precision.HIGHEST,
        ),
        "rep",
        scatter_dimension=0,
        tiled=True,
    )
    weight_part = lax.dot_general(
        features,
        lax.all_gather(grad_mixed, "rep", axis=0, tiled=True),
        (((1,), (1,)), ((), ())),
        precision=lax.Precision.HIGHEST,
        preferred_element_type=jnp.float32,
    )
    node_total = stretch_len * n_rowdev * n_coldev
    weight_grad = lax.psum(weight_part * float(node_total) ** (-0.5), ("row", "col"))
    return (output, input_grad, weight_grad)


def solution(mesh):
    return jax.shard_map(
        local,
        mesh=mesh,
        in_specs=(
            P("rep", ("col", "row")),
            P(),
            P("rep", ("row", "col")),
            P(("row", "col"), None, None),
            P(("row", "col")),
            P(("row", "col")),
            P(("row", "col")),
            P(("row", "col")),
        ),
        out_specs=(P("rep", ("row", "col")), P("rep", ("col", "row")), P("rep", None)),
        check_vma=False,
    )
```

profile of v0, /device:TPU:2, one launch (start us, length us, event | category | flops | bytes accessed | tf_op | source)
XLA Modules:
  0.0 1082.4 jit_solution(2901445615518222513)
XLA Ops:
  7.2 0.0 copy-start
  7.2 0.0 reduce-scatter.5.cloned.1.call-start
  7.2 0.9 copy-done
  8.1 2.3 fusion.39
  10.4 0.0 reduce-scatter.5.cloned.1.call-update
  10.5 0.0 all-gather.3.cloned.1.call-start
  10.5 30.2 %reduce-scatter.5.cloned.1.call-done = f32[64,512]{1,0:T(8,128)} async-done(((f32[256,512]{1,0:T(8,128)}), f32[64,512]{1,0:T(8,128)}) %reduce-scatter.5.cloned.1.call-update) | async-done | bytes 131088 | tf_op jit(solution)/shard_map/reduce_scatter | solution.py:46
  40.7 0.0 all-gather.3.cloned.1.call-update
  40.7 0.0 reduce-scatter.7.cloned.1.call-start
  41.4 0.7 compare_select_fusion.2
  42.1 0.0 copy-start.3
  42.1 0.0 copy-start.5
  42.1 14.2 %gather_fusion = f32[160,128,128]{2,1,0:T(8,128)} fusion(f32[160,128,128]{2,1,0:T(8,128)} %param.15, s32[1024]{0:T(1024)S(1)} %pad_clamp_fusion.2), kind=kCustom, calls=%fused_computation.clone | custom fusion | bytes 20972160 | tf_op jit(solution)/shard_map/jit(_take)/gather | solution.py:12
  56.3 0.0 copy-done.3
  56.3 0.0 copy-done.5
  56.3 10.5 all-gather.3.cloned.1.call-done
  66.8 1.3 copy_bitcast_fusion.3
  68.2 3.3 gather_fusion.1
  71.5 0.0 copy-start.4
  71.5 24.3 %fusion.20 = f32[64,160,128]{2,0,1:T(8,128)S(1)} fusion(f32[160,64,128]{2,1,0:T(8,128)} %gather_fusion.1, pred[160]{0:T(512)(128)(4,1)S(1)} %get-tuple-element.7, f32[160,128,128]{2,1,0:T(8,128)} %gather_fusion, pred[160]{0:T(512)(128)(4,1)S(1)} %get-tuple-element.8), kind=kOutput, calls=%fused_computation.23 | convolution fusion | flops 2017198080 | bytes 20971840 | tf_op jit(solution)/shard_map/fgb,gab->fga/dot_general | solution.py:16
  95.8 0.0 copy-done.4
  95.8 0.0 copy-start.2
  95.8 5.6 fusion.8
  101.5 1.6 copy.29
  103.0 0.0 reduce-scatter.7.cloned.1.call-update
  103.1 0.0 all-gather.5.cloned.1.call-start
  103.1 87.2 %reduce-scatter.7.cloned.1.call-done = f32[64,512]{1,0:T(8,128)} async-done(((f32[64,4096]{1,0:T(8,128)}), f32[64,512]{1,0:T(8,128)}) %reduce-scatter.7.cloned.1.call-update) | async-done | bytes 131088 | tf_op jit(solution)/shard_map/reduce_scatter | solution.py:62
  190.4 0.0 copy-done.2
  190.4 1.7 fusion.36
  192.1 0.0 all-gather.5.cloned.1.call-update
  192.1 0.0 reduce-scatter.9.cloned.1.call-start
  192.2 59.1 %all-gather.5.cloned.1.call-done = f32[64,4096]{1,0:T(8,128)} async-done(((f32[64,512]{1,0:T(8,128)}), f32[64,4096]{1,0:T(8,128)}) %all-gather.5.cloned.1.call-update) | async-done | bytes 1048592 | tf_op jit(solution)/shard_map/all_gather | solution.py:65
  251.3 1.3 copy_bitcast_fusion.2
  252.7 3.3 gather_fusion.2
  255.9 13.9 %fusion.25 = f32[64,160,128]{2,0,1:T(8,128)S(1)} fusion(f32[160,64,128]{2,1,0:T(8,128)} %gather_fusion.2, pred[160]{0:T(512)(128)(4,1)S(1)} %compare_and_fusion, f32[160,128,128]{2,1,0:T(8,128)} %gather_fusion, pred[160]{0:T(512)(128)(4,1)S(1)} %get-tuple-element.8), kind=kOutput, calls=%fused_computation.24 | convolution fusion | flops 2017198080 | bytes 20971840 | tf_op jit(solution)/shard_map/fga,gab->fgb/dot_general | solution.py:14
  269.8 0.0 copy-start.1
  269.8 5.6 fusion.6
  275.5 1.6 copy.28
  277.1 0.0 reduce-scatter.9.cloned.1.call-update
  277.1 0.0 all-reduce.2.cloned.1.call-start
  277.1 30.8 %reduce-scatter.9.cloned.1.call-done = f32[64,512]{1,0:T(8,128)} async-done(((f32[64,4096]{1,0:T(8,128)}), f32[64,512]{1,0:T(8,128)}) %reduce-scatter.9.cloned.1.call-update) | async-done | bytes 131088 | tf_op jit(solution)/shard_map/reduce_scatter | solution.py:69
  307.9 16.4 %all_gather.11 = f32[256,512]{1,0:T(8,128)S(1)} all-gather(f32[64,512]{1,0:T(8,128)} %reduce-scatter.9.cloned.1.call-done), channel_id=1, replica_groups=mesh['row'=8,'col'=8,'rep'=4] {'rep'}, dimensions={0}, use_global_device_ids=true | all-gather | bytes 655360 | tf_op jit(solution)/shard_map/all_gather | solution.py:83
  324.4 0.0 copy-done.1
  324.4 1.2 fusion.30
  325.6 0.0 all-reduce.2.cloned.1.call-update
  325.6 0.0 reduce-scatter.11.cloned.1.call-start
  325.7 2.3 fusion.37
  328.0 0.0 reduce-scatter.11.cloned.1.call-update
  328.0 722.2 %all-reduce.2.cloned.1.call-done = f32[64,256]{1,0:T(8,128)} async-done(((f32[64,256]{1,0:T(8,128)}), f32[64,256]{1,0:T(8,128)}) %all-reduce.2.cloned.1.call-update) | async-done | bytes 65552 | tf_op jit(solution)/shard_map/psum | solution.py:89
  1050.2 23.9 %reduce-scatter.11.cloned.1.call-done = f32[64,512]{1,0:T(8,128)} async-done(((f32[256,512]{1,0:T(8,128)}), f32[64,512]{1,0:T(8,128)}) %reduce-scatter.11.cloned.1.call-update) | async-done | bytes 131088 | tf_op jit(solution)/shard_map/reduce_scatter | solution.py:70
  1074.1 1.5 copy.32
  (8 shorter events, 0.0 us)
Async XLA Ops:
  7.2 1.0 copy-start
  7.2 33.5 %reduce-scatter.5.cloned.1.call-start = ((), (), s32[]{:S(2)}) async-start(), calls=%async_computation.4 | async-start | bytes 655360 | tf_op jit(solution)/shard_map/reduce_scatter | solution.py:46
  10.5 56.4 %all-gather.3.cloned.1.call-start = ((), (), s32[]{:S(2)}) async-start(), calls=%async_computation.5 | async-start | bytes 1179648 | tf_op jit(solution)/shard_map/all_gather | solution.py:58
  40.7 149.7 %reduce-scatter.7.cloned.1.call-start = ((), (), s32[]{:S(2)}) async-start(), calls=%async_computation.6 | async-start | bytes 1179648 | tf_op jit(solution)/shard_map/reduce_scatter | solution.py:62
  42.1 14.2 %copy-start.3 = (s32[160]{0:T(256)S(1)}, s32[160]{0:T(256)}, u32[]{:S(2)}) copy-start(s32[160]{0:T(256)} %param.17) | copy-start | bytes 1924
  42.1 14.2 %copy-start.5 = (s32[160]{0:T(256)S(1)}, s32[160]{0:T(256)}, u32[]{:S(2)}) copy-start(s32[160]{0:T(256)} %param.18) | copy-start | bytes 1924
  71.5 24.3 %copy-start.4 = (s32[160]{0:T(256)S(1)}, s32[160]{0:T(256)}, u32[]{:S(2)}) copy-start(s32[160]{0:T(256)} %param.16) | copy-start | bytes 1924
  95.8 94.6 %copy-start.2 = (f32[64,512]{1,0:T(8,128)S(1)}, f32[64,512]{1,0:T(8,128)}, u32[]{:S(2)}) copy-start(f32[64,512]{1,0:T(8,128)} %param.14) | copy-start | bytes 393220
  103.1 148.2 %all-gather.5.cloned.1.call-start = ((), (), s32[]{:S(2)}) async-start(), calls=%async_computation.7 | async-start | bytes 1179648 | tf_op jit(solution)/shard_map/all_gather | solution.py:65
  192.1 115.8 %reduce-scatter.9.cloned.1.call-start = ((), (), s32[]{:S(2)}) async-start(), calls=%async_computation.8 | async-start | bytes 1179648 | tf_op jit(solution)/shard_map/reduce_scatter | solution.py:69
  269.8 54.5 %copy-start.1 = (f32[64,512]{1,0:T(8,128)S(1)}, f32[64,512]{1,0:T(8,128)}, u32[]{:S(2)}) copy-start(f32[64,512]{1,0:T(8,128)} %param.12) | copy-start | bytes 393220
  277.1 773.1 %all-reduce.2.cloned.1.call-start = ((), (), s32[]{:S(2)}) async-start(), calls=%async_computation.10 | async-start | bytes 131072 | tf_op jit(solution)/shard_map/psum | solution.py:89
  325.6 748.5 %reduce-scatter.11.cloned.1.call-start = ((), (), s32[]{:S(2)}) async-start(), calls=%async_computation.9 | async-start | bytes 655360 | tf_op jit(solution)/shard_map/reduce_scatter | solution.py:70
Sparse Core Ops, SparseCore 0:
  10.6 30.0 reduce-scatter.4
  42.5 24.2 all-gather.2
  103.2 87.1 reduce-scatter.6
  193.4 57.8 all-gather.4
  277.2 30.6 reduce-scatter.8
  325.7 724.4 all-reduce.1
  1053.3 20.7 reduce-scatter.10
where the time goes:
time: 1080 us
  waiting for transfers between devices  964 us (89%)
  matrix products  55.3 us (5%)
  local copies, waits for them, and re-layouts  29 us (3%)
  blocking collectives  16.4 us (2%)
  between operations  14.9 us (1%)
    psum x1, waiting for transfers between devices, local(): lax.psum(weight_part * float(node_total) ** (-0.5), ('row', 'col'))  722 us
    reduce_scatter x1, waiting for transfers between devices, local(): lax.psum_scatter(partial_value, 'col', scatter_dimension=1, tiled=True)  87.2 us
    all_gather x1, waiting for transfers between devices, local(): row_block = lax.all_gather(grad_pre, 'col', axis=1, tiled=True)  59.1 us
    reduce_scatter x1, waiting for transfers between devices, local(): lax.psum_scatter(partial_back, 'row', scatter_dimension=1, tiled=True)  30.8 us
    reduce_scatter x1, waiting for transfers between devices, local(): lax.psum_scatter(lax.dot_general(own_rows, features, (((0,), (0,)), ((),...  30.2 us
    dot_general x1, matrix products, tile_terms(): jnp.einsum('fgb,gab->fga', picked, chosen, precision=lax.Precision.HIGHEST)  24.3 us
    reduce_scatter x1, waiting for transfers between devices, local(): lax.psum_scatter(jnp.dot(own_cols, grad_mixed, preferred_element_type=jnp...  23.9 us
  transfers between devices with their start and end apart: 7, of which 7 were waited for; matrix products, arithmetic and copies ran while one was open for 2% of the time, Pallas kernels for 0%

commit v1 on v0

--- a/solution.py
+++ b/solution.py
@@ -86,7 +86,8 @@
         preferred_element_type=jnp.float32,
     )
     node_total = stretch_len * n_rowdev * n_coldev
-    weight_grad = lax.psum(weight_part * float(node_total) ** (-0.5), ("row", "col"))
+    xx = weight_part * float(node_total) ** (-0.5)
+    weight_grad = lax.psum(lax.psum(xx, axis_name="row"), axis_name="col")
     return (output, input_grad, weight_grad)
 
 

time: 1080 us -> 530 us (0.49)
  waiting for transfers between devices: 964 us -> 411 us
    psum x1 -> x2, waiting for transfers between devices: 722 us -> 167 us  [local(): weight_grad = lax.psum(lax.psum(xx, axis_name='row'), axis_name='col')]
  transfers between devices with their start and end apart: 7 -> 8, of which waited for: 7 -> 8; matrix products, arithmetic and copies ran while one was open for 2% -> 3% of each run, Pallas kernels for 0% -> 0%
where the time goes in v1:
time: 530 us; the launch traced here: 529 us
  waiting for transfers between devices  411 us (78%)
  matrix products  55.3 us (10%)
  local copies, waits for them, and re-layouts  29 us (5%)
  blocking collectives  16.4 us (3%)
  between operations  14.9 us (3%)
    psum x2, waiting for transfers between devices, local(): weight_grad = lax.psum(lax.psum(xx, axis_name='row'), axis_name='col')  167 us
    reduce_scatter x1, waiting for transfers between devices, local(): lax.psum_scatter(partial_value, 'col', scatter_dimension=1, tiled=True)  87.2 us
    all_gather x1, waiting for transfers between devices, local(): row_block = lax.all_gather(grad_pre, 'col', axis=1, tiled=True)  59.1 us
    reduce_scatter x1, waiting for transfers between devices, local(): lax.psum_scatter(partial_back, 'row', scatter_dimension=1, tiled=True)  30.8 us
    reduce_scatter x1, waiting for transfers between devices, local(): lax.psum_scatter(lax.dot_general(own_rows, features, (((0,), (0,)), ((),...  30.2 us
    reduce_scatter x1, waiting for transfers between devices, local(): lax.psum_scatter(jnp.dot(own_cols, grad_mixed, preferred_element_type=jnp...  26.3 us
    dot_general x1, matrix products, tile_terms(): jnp.einsum('fgb,gab->fga', picked, chosen, precision=lax.Precision.HIGHEST)  24.3 us
    all_gather x1, blocking collectives, local(): lax.all_gather(grad_mixed, 'rep', axis=0, tiled=True)  16.4 us
  transfers between devices with their start and end apart: 8, of which 8 were waited for; matrix products, arithmetic and copies ran while one was open for 3% of the time, Pallas kernels for 0%

profile of v1, /device:TPU:2, one launch (start us, length us, event | category | flops | bytes accessed | tf_op | source)
XLA Modules:
  0.0 529.2 jit_solution(2774833966080528476)
XLA Ops:
  7.2 0.0 copy-start
  7.2 0.0 reduce-scatter.5.cloned.1.call-start
  7.2 0.9 copy-done
  8.1 2.3 fusion.39
  10.4 0.0 reduce-scatter.5.cloned.1.call-update
  10.5 0.0 all-gather.3.cloned.1.call-start
  10.5 30.2 %reduce-scatter.5.cloned.1.call-done = f32[64,512]{1,0:T(8,128)} async-done(((f32[256,512]{1,0:T(8,128)}), f32[64,512]{1,0:T(8,128)}) %reduce-scatter.5.cloned.1.call-update) | async-done | bytes 131088 | tf_op jit(solution)/shard_map/reduce_scatter | solution.py:46
  40.7 0.0 all-gather.3.cloned.1.call-update
  40.7 0.0 reduce-scatter.7.cloned.1.call-start
  41.4 0.7 compare_select_fusion.2
  42.1 0.0 copy-start.3
  42.1 0.0 copy-start.5
  42.1 14.2 %gather_fusion = f32[160,128,128]{2,1,0:T(8,128)} fusion(f32[160,128,128]{2,1,0:T(8,128)} %param.15, s32[1024]{0:T(1024)S(1)} %pad_clamp_fusion.2), kind=kCustom, calls=%fused_computation.clone | custom fusion | bytes 20972160 | tf_op jit(solution)/shard_map/jit(_take)/gather | solution.py:12
  56.3 0.0 copy-done.3
  56.3 0.0 copy-done.5
  56.3 10.5 %all-gather.3.cloned.1.call-done = f32[64,4096]{1,0:T(8,128)} async-done(((f32[64,512]{1,0:T(8,128)}), f32[64,4096]{1,0:T(8,128)}) %all-gather.3.cloned.1.call-update) | async-done | bytes 1048592 | tf_op jit(solution)/shard_map/all_gather | solution.py:58
  66.8 1.3 copy_bitcast_fusion.3
  68.2 3.3 gather_fusion.1
  71.5 0.0 copy-start.4
  71.5 24.3 %fusion.20 = f32[64,160,128]{2,0,1:T(8,128)S(1)} fusion(f32[160,64,128]{2,1,0:T(8,128)} %gather_fusion.1, pred[160]{0:T(512)(128)(4,1)S(1)} %get-tuple-element.7, f32[160,128,128]{2,1,0:T(8,128)} %gather_fusion, pred[160]{0:T(512)(128)(4,1)S(1)} %get-tuple-element.8), kind=kOutput, calls=%fused_computation.23 | convolution fusion | flops 2017198080 | bytes 20971840 | tf_op jit(solution)/shard_map/fgb,gab->fga/dot_general | solution.py:16
  95.8 0.0 copy-done.4
  95.8 0.0 copy-start.2
  95.8 5.6 %fusion.8 = f32[32,64,128]{2,0,1:T(8,128)S(1)} fusion(f32[64,160,128]{2,0,1:T(8,128)S(1)} %fusion.20, f32[160]{0:T(256)S(1)} %compare_convert_fusion, s32[160]{0:T(256)S(1)} %copy-done.4), kind=kOutput, calls=%fused_computation.11 | convolution fusion | flops 503326720 | bytes 6292736 | tf_op jit(solution)/shard_map/fgt,gd->fdt/dot_general | solution.py:21
  101.5 1.6 copy.29
  103.0 0.0 reduce-scatter.7.cloned.1.call-update
  103.1 0.0 all-gather.5.cloned.1.call-start
  103.1 87.2 %reduce-scatter.7.cloned.1.call-done = f32[64,512]{1,0:T(8,128)} async-done(((f32[64,4096]{1,0:T(8,128)}), f32[64,512]{1,0:T(8,128)}) %reduce-scatter.7.cloned.1.call-update) | async-done | bytes 131088 | tf_op jit(solution)/shard_map/reduce_scatter | solution.py:62
  190.4 0.0 copy-done.2
  190.4 1.7 fusion.36
  192.1 0.0 all-gather.5.cloned.1.call-update
  192.1 0.0 reduce-scatter.9.cloned.1.call-start
  192.2 59.1 %all-gather.5.cloned.1.call-done = f32[64,4096]{1,0:T(8,128)} async-done(((f32[64,512]{1,0:T(8,128)}), f32[64,4096]{1,0:T(8,128)}) %all-gather.5.cloned.1.call-update) | async-done | bytes 1048592 | tf_op jit(solution)/shard_map/all_gather | solution.py:65
  251.3 1.3 copy_bitcast_fusion.2
  252.7 3.3 gather_fusion.2
  255.9 13.9 %fusion.25 = f32[64,160,128]{2,0,1:T(8,128)S(1)} fusion(f32[160,64,128]{2,1,0:T(8,128)} %gather_fusion.2, pred[160]{0:T(512)(128)(4,1)S(1)} %compare_and_fusion, f32[160,128,128]{2,1,0:T(8,128)} %gather_fusion, pred[160]{0:T(512)(128)(4,1)S(1)} %get-tuple-element.8), kind=kOutput, calls=%fused_computation.24 | convolution fusion | flops 2017198080 | bytes 20971840 | tf_op jit(solution)/shard_map/fga,gab->fgb/dot_general | solution.py:14
  269.8 0.0 copy-start.1
  269.8 5.6 %fusion.6 = f32[32,64,128]{2,0,1:T(8,128)S(1)} fusion(f32[64,160,128]{2,0,1:T(8,128)S(1)} %fusion.25, s32[160]{0:T(256)S(1)} %copy-done.3, f32[160]{0:T(256)S(1)} %compare_convert_fusion), kind=kOutput, calls=%fused_computation.9 | convolution fusion | flops 503326720 | bytes 6292736 | tf_op jit(solution)/shard_map/fgt,gd->fdt/dot_general | solution.py:21
  275.5 1.6 copy.28
  277.1 0.0 reduce-scatter.9.cloned.1.call-update
  277.1 0.0 all-reduce.3.cloned.1.call-start
  277.1 30.8 %reduce-scatter.9.cloned.1.call-done = f32[64,512]{1,0:T(8,128)} async-done(((f32[64,4096]{1,0:T(8,128)}), f32[64,512]{1,0:T(8,128)}) %reduce-scatter.9.cloned.1.call-update) | async-done | bytes 131088 | tf_op jit(solution)/shard_map/reduce_scatter | solution.py:69
  307.9 16.4 %all_gather.11 = f32[256,512]{1,0:T(8,128)S(1)} all-gather(f32[64,512]{1,0:T(8,128)} %reduce-scatter.9.cloned.1.call-done), channel_id=1, replica_groups=mesh['row'=8,'col'=8,'rep'=4] {'rep'}, dimensions={0}, use_global_device_ids=true | all-gather | bytes 655360 | tf_op jit(solution)/shard_map/all_gather | solution.py:83
  324.4 0.0 copy-done.1
  324.4 1.2 fusion.30
  325.6 0.0 all-reduce.3.cloned.1.call-update
  325.6 0.0 all-reduce.5.cloned.1.call-start
  325.7 62.8 %all-reduce.3.cloned.1.call-done = f32[64,256]{1,0:T(8,128)} async-done(((f32[64,256]{1,0:T(8,128)}), f32[64,256]{1,0:T(8,128)}) %all-reduce.3.cloned.1.call-update) | async-done | bytes 65552 | tf_op jit(solution)/shard_map/psum | solution.py:90
  388.5 0.0 all-reduce.5.cloned.1.call-update
  388.5 0.0 reduce-scatter.11.cloned.1.call-start
  388.6 2.3 fusion.37
  390.9 0.0 reduce-scatter.11.cloned.1.call-update
  390.9 103.7 %all-reduce.5.cloned.1.call-done = f32[64,256]{1,0:T(8,128)} async-done(((f32[64,256]{1,0:T(8,128)}), f32[64,256]{1,0:T(8,128)}) %all-reduce.5.cloned.1.call-update) | async-done | bytes 65552 | tf_op jit(solution)/shard_map/psum | solution.py:90
  494.6 26.3 %reduce-scatter.11.cloned.1.call-done = f32[64,512]{1,0:T(8,128)} async-done(((f32[256,512]{1,0:T(8,128)}), f32[64,512]{1,0:T(8,128)}) %reduce-scatter.11.cloned.1.call-update) | async-done | bytes 131088 | tf_op jit(solution)/shard_map/reduce_scatter | solution.py:70
  520.9 1.5 copy.33
  (8 shorter events, 0.0 us)
Async XLA Ops:
  7.2 1.0 copy-start
  7.2 33.5 %reduce-scatter.5.cloned.1.call-start = ((), (), s32[]{:S(2)}) async-start(), calls=%async_computation.4 | async-start | bytes 655360 | tf_op jit(solution)/shard_map/reduce_scatter | solution.py:46
  10.5 56.4 %all-gather.3.cloned.1.call-start = ((), (), s32[]{:S(2)}) async-start(), calls=%async_computation.5 | async-start | bytes 1179648 | tf_op jit(solution)/shard_map/all_gather | solution.py:58
  40.7 149.7 %reduce-scatter.7.cloned.1.call-start = ((), (), s32[]{:S(2)}) async-start(), calls=%async_computation.6 | async-start | bytes 1179648 | tf_op jit(solution)/shard_map/reduce_scatter | solution.py:62
  42.1 14.2 %copy-start.3 = (s32[160]{0:T(256)S(1)}, s32[160]{0:T(256)}, u32[]{:S(2)}) copy-start(s32[160]{0:T(256)} %param.17) | copy-start | bytes 1924
  42.1 14.2 %copy-start.5 = (s32[160]{0:T(256)S(1)}, s32[160]{0:T(256)}, u32[]{:S(2)}) copy-start(s32[160]{0:T(256)} %param.18) | copy-start | bytes 1924
  71.5 24.3 %copy-start.4 = (s32[160]{0:T(256)S(1)}, s32[160]{0:T(256)}, u32[]{:S(2)}) copy-start(s32[160]{0:T(256)} %param.16) | copy-start | bytes 1924
  95.8 94.6 %copy-start.2 = (f32[64,512]{1,0:T(8,128)S(1)}, f32[64,512]{1,0:T(8,128)}, u32[]{:S(2)}) copy-start(f32[64,512]{1,0:T(8,128)} %param.14) | copy-start | bytes 393220
  103.1 148.2 %all-gather.5.cloned.1.call-start = ((), (), s32[]{:S(2)}) async-start(), calls=%async_computation.7 | async-start | bytes 1179648 | tf_op jit(solution)/shard_map/all_gather | solution.py:65
  192.1 115.8 %reduce-scatter.9.cloned.1.call-start = ((), (), s32[]{:S(2)}) async-start(), calls=%async_computation.8 | async-start | bytes 1179648 | tf_op jit(solution)/shard_map/reduce_scatter | solution.py:69
  269.8 54.5 %copy-start.1 = (f32[64,512]{1,0:T(8,128)S(1)}, f32[64,512]{1,0:T(8,128)}, u32[]{:S(2)}) copy-start(f32[64,512]{1,0:T(8,128)} %param.12) | copy-start | bytes 393220
  277.1 111.4 %all-reduce.3.cloned.1.call-start = ((), (), s32[]{:S(2)}) async-start(), calls=%async_computation.10 | async-start | bytes 131072 | tf_op jit(solution)/shard_map/psum | solution.py:90
  325.6 169.0 %all-reduce.5.cloned.1.call-start = ((), (), s32[]{:S(2)}) async-start(), calls=%async_computation.11 | async-start | bytes 131072 | tf_op jit(solution)/shard_map/psum | solution.py:90
  388.5 132.4 %reduce-scatter.11.cloned.1.call-start = ((), (), s32[]{:S(2)}) async-start(), calls=%async_computation.9 | async-start | bytes 655360 | tf_op jit(solution)/shard_map/reduce_scatter | solution.py:70
Sparse Core Ops, SparseCore 0:
  10.6 30.0 reduce-scatter.4
  42.5 24.2 all-gather.2
  103.2 87.1 reduce-scatter.6
  193.4 57.8 all-gather.4
  277.2 30.6 reduce-scatter.8
  325.7 62.7 all-reduce.2
  391.1 103.4 all-reduce.4
  497.7 23.1 reduce-scatter.10
